TPU v7x, 256 devices: a whole 4x4x8 slice. The times are simulated.
256 devices in a mesh: dp: 32 (over z, y_hi, core), expert: 8 (over x, y_lo).
Axes of the slice: x: 4, y: 4 (y_hi: 2, y_lo: 2; y = y_hi * 2 + y_lo), z: 8, core: 2. Of those that a mesh axis runs over, the one named last changes fastest.
Arguments:
- tokens: bfloat16 [32768, 2048], P(('dp', 'expert')), may hold values from -24 to 24
- cotangent: bfloat16 [32768, 2048], P(('dp', 'expert')), may hold values from -24 to 24
- expert_ids: int32 [32768, 2], P(('dp', 'expert')), may hold values from 0 to 7, all different within a row; in each aligned block of 128 rows (0 to 127, 128 to 255, ...) at most 40 rows name the same one
- gate_weights: float32 [32768, 2], P(('dp', 'expert')), may hold values from 0.1 to 1
- partner: int32 [8], replicated, may hold values from 0 to 7, as said below
- w_gate: bfloat16 [8, 2048, 768], P('expert'), may hold values from -0.125 to 0.125
- w_up: bfloat16 [8, 2048, 768], P('expert'), may hold values from -0.125 to 0.125
- w_down: bfloat16 [8, 768, 2048], P('expert'), may hold values from -0.21875 to 0.21875
Outputs:
- mixed_out: bfloat16 [32768, 2048], P(('dp', 'expert'))
- token_grad: bfloat16 [32768, 2048], P(('dp', 'expert'))
- gate_grad: float32 [32768, 2], P(('dp', 'expert'))
- slot_grad_gate: float32 [8, 2048, 768], P('expert', 'dp')
- slot_grad_up: float32 [8, 2048, 768], P('expert', 'dp')
- slot_grad_down: float32 [8, 768, 2048], P('expert', None, 'dp')
Inputs may be any that keep to these rules, and one draw needn't show every extreme that they name: `expert_ids`: each row names 2 different experts. Among the 128 rows of one device no expert is named by more than 40 rows, and in every draw some device names some expert exactly 40 times. partner[partner[i]] = i and partner[i] != i for every slot i.
All inputs are finite; a program needn't handle non-finite values.
Results may differ from a plain program's by a relative error of at most 0.015.
Values may be sent and summed in bfloat16 or wider, within the bound.
A program may use at most 128 MiB of HBM per device.

v0:
```python
import jax
import jax.numpy as jnp
from jax import lax
from jax.sharding import PartitionSpec as P


def as_sent(shard):

    def short(part):
        return part.astype(jnp.bfloat16) if part.dtype == jnp.float32 else part

    return jax.tree.map(short, shard)


def contract_rows(left_mat, right_mat):
    return lax.dot_general(
        left_mat, right_mat, (((0,), (0,)), ((), ())), preferred_element_type=jnp.float32
    )


def contract_cols(left_mat, right_mat):
    return lax.dot_general(
        left_mat, right_mat, (((1,), (1,)), ((), ())), preferred_element_type=jnp.float32
    )


def pick_from(stacked, source):
    return lax.dynamic_index_in_dim(stacked, source, 0, keepdims=False)


def shards(tokens, cotangent, expert_ids, gate_weights, partner, w_gate, w_up, w_down):
    groups = lax.axis_size("expert")
    my_group = lax.axis_index("expert")
    tok_count, model_width = tokens.shape
    top_count = expert_ids.shape[1]
    capacity = min(tok_count, 5 * tok_count * top_count // (4 * groups))
    buffer_rows = groups * capacity
    group_ids = jnp.arange(groups, dtype=jnp.int32)
    my_mate = pick_from(partner, my_group)
    flat_ids = expert_ids.reshape(-1)
    dest_group = jnp.sum(
        jnp.where(flat_ids[:, None] == group_ids[None, :], partner[None, :], 0), axis=1
    )
    one_hot = (dest_group[:, None] == group_ids[None, :]).astype(jnp.int32)
    earlier = jnp.cumsum(one_hot, axis=0) - one_hot
    slot_index = dest_group * capacity + jnp.sum(earlier * one_hot, axis=1)
    place_mat = (slot_index[None, :] == jnp.arange(buffer_rows, dtype=jnp.int32)[:, None]).astype(
        jnp.bfloat16
    )
    replicas = lax.axis_size("dp")
    share_rows = model_width // replicas
    share_start = lax.axis_index("dp") * share_rows
    shares = (
        lax.dynamic_slice_in_dim(w_gate[0], share_start, share_rows, 0),
        lax.dynamic_slice_in_dim(w_up[0], share_start, share_rows, 0),
        lax.dynamic_slice_in_dim(w_down[0], share_start, share_rows, 1),
    )
    is_mate = (partner == my_group)[:, None, None]
    outgoing = tuple(
        (
            jnp.where(is_mate, own_share[None], jnp.zeros_like(own_share)[None])
            for own_share in shares
        )
    )
    incoming = jax.tree.map(
        lambda part, own: part.astype(own.dtype),
        lax.all_to_all(as_sent(outgoing), "expert", split_axis=0, concat_axis=0, tiled=True),
        outgoing,
    )
    mate_shares = tuple((pick_from(block_piece, my_mate) for block_piece in incoming))
    gate_mat, up_mat, down_mat = (
        lax.all_gather(mate_shares[0], "dp", axis=0, tiled=True),
        lax.all_gather(mate_shares[1], "dp", axis=0, tiled=True),
        lax.all_gather(mate_shares[2], "dp", axis=1, tiled=True),
    )
    repeated = jnp.repeat(tokens, top_count, axis=0)
    outgoing_rows = jnp.dot(place_mat, repeated, preferred_element_type=jnp.float32).astype(
        jnp.bfloat16
    )
    expert_in = lax.all_to_all(
        outgoing_rows.reshape(groups, capacity, model_width),
        "expert",
        split_axis=0,
        concat_axis=0,
        tiled=True,
    ).reshape(buffer_rows, model_width)
    gate_pre = jnp.dot(expert_in, gate_mat, preferred_element_type=jnp.float32)
    up_pre = jnp.dot(expert_in, up_mat, preferred_element_type=jnp.float32)
    sigmoid_gate = jax.nn.sigmoid(gate_pre)
    hidden = (gate_pre * sigmoid_gate * up_pre).astype(jnp.bfloat16)
    expert_out = jnp.dot(hidden, down_mat, preferred_element_type=jnp.float32).astype(jnp.bfloat16)
    returned = lax.all_to_all(
        expert_out.reshape(groups, capacity, model_width),
        "expert",
        split_axis=0,
        concat_axis=0,
        tiled=True,
    ).reshape(buffer_rows, model_width)
    per_assign = (
        jnp.take(returned, slot_index, axis=0)
        .astype(jnp.float32)
        .reshape(tok_count, top_count, model_width)
    )
    mixed_out = jnp.sum(gate_weights[:, :, None] * per_assign, axis=1).astype(jnp.bfloat16)
    cot_float = cotangent.astype(jnp.float32)
    gate_grad = jnp.sum(cot_float[:, None, :] * per_assign, axis=2)
    scaled = (
        (gate_weights[:, :, None] * cot_float[:, None, :])
        .astype(jnp.bfloat16)
        .reshape(-1, model_width)
    )
    outgoing_grads = jnp.dot(place_mat, scaled, preferred_element_type=jnp.float32).astype(
        jnp.bfloat16
    )
    grads_in = lax.all_to_all(
        outgoing_grads.reshape(groups, capacity, model_width),
        "expert",
        split_axis=0,
        concat_axis=0,
        tiled=True,
    ).reshape(buffer_rows, model_width)
    hidden_grad = contract_cols(grads_in, down_mat)
    gate_grad_pre = (
        hidden_grad * up_pre * sigmoid_gate * (1.0 + gate_pre * (1.0 - sigmoid_gate))
    ).astype(jnp.bfloat16)
    up_grad_pre = (hidden_grad * gate_pre * sigmoid_gate).astype(jnp.bfloat16)
    row_grad = (contract_cols(gate_grad_pre, gate_mat) + contract_cols(up_grad_pre, up_mat)).astype(
        jnp.bfloat16
    )
    returned_grads = lax.all_to_all(
        row_grad.reshape(groups, capacity, model_width),
        "expert",
        split_axis=0,
        concat_axis=0,
        tiled=True,
    ).reshape(buffer_rows, model_width)
    grad_rows = (
        jnp.take(returned_grads, slot_index, axis=0)
        .astype(jnp.float32)
        .reshape(tok_count, top_count, model_width)
    )
    token_grad = jnp.sum(grad_rows, axis=1).astype(jnp.bfloat16)
    partial_gate = contract_rows(expert_in, gate_grad_pre)
    partial_up = contract_rows(expert_in, up_grad_pre)
    partial_down = contract_rows(hidden, grads_in)
    sum_gate, sum_up, sum_down = (
        lax.psum_scatter(
            partial_gate.astype(jnp.bfloat16), "dp", scatter_dimension=0, tiled=True
        ).astype(jnp.float32),
        lax.psum_scatter(
            partial_up.astype(jnp.bfloat16), "dp", scatter_dimension=0, tiled=True
        ).astype(jnp.float32),
        lax.psum_scatter(
            partial_down.astype(jnp.bfloat16), "dp", scatter_dimension=1, tiled=True
        ).astype(jnp.float32),
    )
    return (mixed_out, token_grad, gate_grad, sum_gate[None], sum_up[None], sum_down[None])


def solution(mesh):
    in_specs = (
        P(("dp", "expert"), None),
        P(("dp", "expert"), None),
        P(("dp", "expert"), None),
        P(("dp", "expert"), None),
        P(),
        P("expert", None, None),
        P("expert", None, None),
        P("expert", None, None),
    )
    out_specs = (
        P(("dp", "expert"), None),
        P(("dp", "expert"), None),
        P(("dp", "expert"), None),
        P("expert", "dp", None),
        P("expert", "dp", None),
        P("expert", None, "dp"),
    )
    return jax.shard_map(shards, mesh=mesh, in_specs=in_specs, out_specs=out_specs, check_vma=False)
```

profile of v0, /device:TPU:4, one launch (start us, length us, event | category | flops | bytes accessed | tf_op | source)
XLA Modules:
  0.0 688.2 jit_solution(8233593337685913203)
XLA Ops:
  10.5 6.3 all-to-all-start.2
  19.3 7.3 %all-to-all-done.2 = bf16[8,64,768]{2,1,0:T(8,128)(2,1)} async-done(((bf16[8,64,768]{2,1,0:T(8,128)(2,1)}), bf16[8,64,768]{2,1,0:T(8,128)(2,1)}, u32[]{:S(2)}, u32[]{:S(2)}) %all-to-all-start.2) | async-done | bytes 786464 | tf_op jit(solution)/shard_map/all_to_all | solution.py:67
  28.7 15.4 %all_to_all.35 = bf16[8,768,64]{1,2,0:T(8,128)(2,1)S(1)} all-to-all(bf16[8,768,64]{1,2,0:T(8,128)(2,1)S(1)} %broadcast_select_fusion.1), channel_id=1, replica_groups=mesh['dp'=32,'expert'=8] {'expert'}, dimensions={0} | all-to-all | bytes 1572864 | tf_op jit(solution)/shard_map/all_to_all | solution.py:67
  44.8 13.8 %all_to_all.36 = bf16[8,64,768]{2,1,0:T(8,128)(2,1)S(1)} all-to-all(bf16[8,64,768]{2,1,0:T(8,128)(2,1)S(1)} %copy-done.6), channel_id=1, replica_groups=mesh['dp'=32,'expert'=8] {'expert'}, dimensions={0} | all-to-all | bytes 1572864 | tf_op jit(solution)/shard_map/all_to_all | solution.py:67
  63.2 6.2 all-to-all-start
  69.5 2.4 mul.83
  71.9 2.7 mul.84
  76.5 6.3 all-to-all-done
  82.8 7.1 %all-to-all-start.5 = ((bf16[8,40,2048]{2,1,0:T(8,128)(2,1)}), bf16[8,40,2048]{2,1,0:T(8,128)(2,1)}, u32[]{:S(2)}, u32[]{:S(2)}) async-start(bf16[8,40,2048]{2,1,0:T(8,128)(2,1)} %bitcast.70), calls=%async_computation.5 | async-start | bytes 2621440 | tf_op jit(solution)/shard_map/all_to_all | solution.py:115
  89.9 34.6 %all-gather.9.cloned.1.call-done = bf16[1,2048,768]{2,1,0:T(8,128)(2,1)} async-done(((bf16[1,64,768]{2,1,0:T(8,128)(2,1)}), bf16[1,2048,768]{2,1,0:T(8,128)(2,1)}) %all-gather.9.cloned.1.call-update) | async-done | bytes 3145744 | tf_op jit(solution)/shard_map/all_gather | solution.py:73
  124.5 3.5 fusion.6
  128.0 79.0 %all-gather.11.cloned.1.call-done = bf16[1,768,2048]{1,2,0:T(8,128)(2,1)} async-done(((bf16[1,768,64]{1,2,0:T(8,128)(2,1)}), bf16[1,768,2048]{1,2,0:T(8,128)(2,1)}) %all-gather.11.cloned.1.call-update) | async-done | bytes 3145744 | tf_op jit(solution)/shard_map/all_gather | solution.py:74
  206.9 3.5 fusion
  210.4 79.6 %all-gather.7.cloned.1.call-done = bf16[1,2048,768]{2,1,0:T(8,128)(2,1)} async-done(((bf16[1,64,768]{2,1,0:T(8,128)(2,1)}), bf16[1,2048,768]{2,1,0:T(8,128)(2,1)}) %all-gather.7.cloned.1.call-update) | async-done | bytes 3145744 | tf_op jit(solution)/shard_map/all_gather | solution.py:72
  290.0 3.7 multiply_convert_fusion.3
  294.5 4.8 convolution_convert_fusion
  299.6 4.9 convolution_convert_fusion.1
  304.5 4.8 convolution_convert_fusion.2
  309.4 3.3 fusion.4
  315.1 5.0 all-to-all-start.6
  320.0 4.3 fusion.18
  324.3 12.7 %all-to-all-done.6 = bf16[8,40,2048]{2,1,0:T(8,128)(2,1)S(1)} async-done(((bf16[8,40,2048]{2,1,0:T(8,128)(2,1)}), bf16[8,40,2048]{2,1,0:T(8,128)(2,1)S(1)}, u32[]{:S(2)}, u32[]{:S(2)}) %all-to-all-start.6) | async-done | bytes 1310752 | tf_op jit(solution)/shard_map/all_to_all | solution.py:130
  337.0 7.2 %all-to-all-start.4 = ((bf16[8,40,2048]{2,1,0:T(8,128)(2,1)}), bf16[8,40,2048]{2,1,0:T(8,128)(2,1)S(1)}, u32[]{:S(2)}, u32[]{:S(2)}) async-start(bf16[8,40,2048]{2,1,0:T(8,128)(2,1)} %bitcast.71), calls=%async_computation.4 | async-start | bytes 2621440 | tf_op jit(solution)/shard_map/all_to_all | solution.py:92
  344.2 2.3 gather_fusion.1
  346.5 15.8 %all-to-all-done.4 = bf16[8,40,2048]{2,1,0:T(8,128)(2,1)S(1)} async-done(((bf16[8,40,2048]{2,1,0:T(8,128)(2,1)}), bf16[8,40,2048]{2,1,0:T(8,128)(2,1)S(1)}, u32[]{:S(2)}, u32[]{:S(2)}) %all-to-all-start.4) | async-done | bytes 1310752 | tf_op jit(solution)/shard_map/all_to_all | solution.py:92
  363.7 2.9 broadcast_select_fusion
  368.8 2.7 reshape.102
  372.7 4.7 reduce.1
  377.5 5.6 multiply_reduce_fusion.1
  383.1 45.0 %reduce-scatter.8.cloned.1.call-done = bf16[768,64]{0,1:T(8,128)(2,1)} async-done(((bf16[768,2048]{0,1:T(8,128)(2,1)}), bf16[768,64]{0,1:T(8,128)(2,1)}) %reduce-scatter.8.cloned.1.call-update) | async-done | bytes 98320 | tf_op jit(solution)/shard_map/reduce_scatter | solution.py:153
  429.7 124.2 %reduce-scatter.6.cloned.1.call-done = bf16[64,768]{1,0:T(8,128)(2,1)} async-done(((bf16[2048,768]{1,0:T(8,128)(2,1)}), bf16[64,768]{1,0:T(8,128)(2,1)}) %reduce-scatter.6.cloned.1.call-update) | async-done | bytes 98320 | tf_op jit(solution)/shard_map/reduce_scatter | solution.py:150
  555.5 124.2 %reduce-scatter.4.cloned.1.call-done = bf16[64,768]{1,0:T(8,128)(2,1)} async-done(((bf16[2048,768]{1,0:T(8,128)(2,1)}), bf16[64,768]{1,0:T(8,128)(2,1)}) %reduce-scatter.4.cloned.1.call-update) | async-done | bytes 98320 | tf_op jit(solution)/shard_map/reduce_scatter | solution.py:147
  (84 shorter events, 26.0 us)
Async XLA Ops:
  7.2 21.0 %copy-start = (bf16[1,768,2048]{2,1,0:T(8,128)(2,1)S(1)}, bf16[1,768,2048]{2,1,0:T(8,128)(2,1)}, u32[]{:S(2)}) copy-start(bf16[1,768,2048]{2,1,0:T(8,128)(2,1)} %param.17) | copy-start | bytes 9437188
  7.2 9.6 %copy-start.11 = (s32[8]{0:T(128)S(1)}, s32[8]{0:T(128)}, u32[]{:S(2)}) copy-start(s32[8]{0:T(128)} %param.14) | copy-start | bytes 100
  10.5 16.1 %all-to-all-start.2 = ((bf16[8,64,768]{2,1,0:T(8,128)(2,1)}), bf16[8,64,768]{2,1,0:T(8,128)(2,1)}, u32[]{:S(2)}, u32[]{:S(2)}) async-start(bf16[8,64,768]{2,1,0:T(8,128)(2,1)} %get-tuple-element.33), calls=%async_computation.2 | async-start | bytes 1572864 | tf_op jit(solution)/shard_map/all_to_all | solution.py:67
  16.8 107.7 %all-gather.9.cloned.1.call-start = ((), (), s32[]{:S(2)}) async-start(), calls=%async_computation.14 | async-start | bytes 3244032 | tf_op jit(solution)/shard_map/all_gather | solution.py:73
  28.2 178.8 %all-gather.11.cloned.1.call-start = ((), (), s32[]{:S(2)}) async-start(), calls=%async_computation.15 | async-start | bytes 3244032 | tf_op jit(solution)/shard_map/all_gather | solution.py:74
  28.4 16.4 %copy-start.6 = (bf16[8,64,768]{2,1,0:T(8,128)(2,1)S(1)}, bf16[8,64,768]{2,1,0:T(8,128)(2,1)}, u32[]{:S(2)}) copy-start(bf16[8,64,768]{2,1,0:T(8,128)(2,1)} %get-tuple-element.32) | copy-start | bytes 2359300
  28.5 30.8 %copy-start.9 = (s32[128,2]{0,1:T(2,128)S(1)}, s32[128,2]{0,1:T(2,128)}, u32[]{:S(2)}) copy-start(s32[128,2]{0,1:T(2,128)} %param.12) | copy-start | bytes 3076
  28.6 31.8 %copy-start.7 = (bf16[128,2048]{1,0:T(8,128)(2,1)S(1)}, bf16[128,2048]{1,0:T(8,128)(2,1)}, u32[]{:S(2)}) copy-start(bf16[128,2048]{1,0:T(8,128)(2,1)} %param.10) | copy-start | bytes 1572868
  44.7 245.3 %all-gather.7.cloned.1.call-start = ((), (), s32[]{:S(2)}) async-start(), calls=%async_computation.13 | async-start | bytes 3244032 | tf_op jit(solution)/shard_map/all_gather | solution.py:72
  61.7 7.8 %copy-start.8 = (bf16[128,2048]{1,0:T(8,128)(2,1)S(1)}, bf16[128,2048]{1,0:T(8,128)(2,1)}, u32[]{:S(2)}) copy-start(bf16[128,2048]{1,0:T(8,128)(2,1)} %param.11) | copy-start | bytes 1572868
  63.2 19.6 %all-to-all-start = ((bf16[8,40,2048]{2,1,0:T(8,128)(2,1)}), bf16[8,40,2048]{2,1,0:T(8,128)(2,1)}, u32[]{:S(2)}, u32[]{:S(2)}) async-start(bf16[8,40,2048]{2,1,0:T(8,128)(2,1)} %bitcast.3), calls=%async_computation | async-start | bytes 2621440 | tf_op jit(solution)/shard_map/all_to_all | solution.py:80
  71.9 2.7 copy-start.10
  74.6 8.2 %copy-start.2 = (f32[256,2048]{1,0:T(8,128)}, f32[256,2048]{1,0:T(8,128)S(1)}, u32[]{:S(2)}) copy-start(f32[256,2048]{1,0:T(8,128)S(1)} %mul.84) | copy-start | bytes 6291460
  82.8 45.1 %all-to-all-start.5 = ((bf16[8,40,2048]{2,1,0:T(8,128)(2,1)}), bf16[8,40,2048]{2,1,0:T(8,128)(2,1)}, u32[]{:S(2)}, u32[]{:S(2)}) async-start(bf16[8,40,2048]{2,1,0:T(8,128)(2,1)} %bitcast.70), calls=%async_computation.5 | async-start | bytes 2621440 | tf_op jit(solution)/shard_map/all_to_all | solution.py:115
  89.9 338.3 %reduce-scatter.8.cloned.1.call-start = ((), (), s32[]{:S(2)}) async-start(), calls=%async_computation.12 | async-start | bytes 3244032 | tf_op jit(solution)/shard_map/reduce_scatter | solution.py:153
  293.7 0.8 copy-start.15
  293.7 10.8 %copy-start.13 = (bf16[320,768]{1,0:T(8,128)(2,1)}, bf16[320,768]{1,0:T(8,128)(2,1)S(1)}, u32[]{:S(2)}) copy-start(bf16[320,768]{1,0:T(8,128)(2,1)S(1)} %get-tuple-element.27) | copy-start | bytes 1474564
  299.4 254.6 %reduce-scatter.6.cloned.1.call-start = ((), (), s32[]{:S(2)}) async-start(), calls=%async_computation.11 | async-start | bytes 3244032 | tf_op jit(solution)/shard_map/reduce_scatter | solution.py:150
  304.5 375.3 %reduce-scatter.4.cloned.1.call-start = ((), (), s32[]{:S(2)}) async-start(), calls=%async_computation.10 | async-start | bytes 3244032 | tf_op jit(solution)/shard_map/reduce_scatter | solution.py:147
  309.4 3.3 copy-start.12
  309.4 3.3 copy-start.14
  315.1 5.0 copy-start.16
  315.1 21.9 %all-to-all-start.6 = ((bf16[8,40,2048]{2,1,0:T(8,128)(2,1)}), bf16[8,40,2048]{2,1,0:T(8,128)(2,1)S(1)}, u32[]{:S(2)}, u32[]{:S(2)}) async-start(bf16[8,40,2048]{2,1,0:T(8,128)(2,1)} %bitcast.16), calls=%async_computation.6 | async-start | bytes 2621440 | tf_op jit(solution)/shard_map/all_to_all | solution.py:130
  337.0 25.4 %all-to-all-start.4 = ((bf16[8,40,2048]{2,1,0:T(8,128)(2,1)}), bf16[8,40,2048]{2,1,0:T(8,128)(2,1)S(1)}, u32[]{:S(2)}, u32[]{:S(2)}) async-start(bf16[8,40,2048]{2,1,0:T(8,128)(2,1)} %bitcast.71), calls=%async_computation.4 | async-start | bytes 2621440 | tf_op jit(solution)/shard_map/all_to_all | solution.py:92
  363.7 2.9 copy-start.4
  366.6 4.9 copy-start.5
  368.8 2.7 copy-start.3
  372.7 308.6 %copy-start.1 = (bf16[1,768,2048]{2,1,0:T(8,128)(2,1)S(1)}, bf16[1,768,2048]{2,1,0:T(8,128)(2,1)}, u32[]{:S(2)}) copy-start(bf16[1,768,2048]{2,1,0:T(8,128)(2,1)} %param.17) | copy-start | bytes 9437188
Sparse Core Ops, SparseCore 0:
  28.3 96.1 all-gather.8
  127.8 79.0 all-gather.10
  210.3 79.6 all-gather.6
  299.5 128.6 reduce-scatter.7
  432.2 121.7 reduce-scatter.5
  558.0 121.7 reduce-scatter.3
where the time goes:
time: 689 us; the launch traced here: 688 us
  waiting for transfers between devices  529 us (77%)
  matrix products  38.3 us (6%)
  starting transfers between devices  32.2 us (5%)
  blocking collectives  29.2 us (4%)
  local copies, waits for them, and re-layouts  21.9 us (3%)
  other arithmetic  21.5 us (3%)
  between operations  16.3 us (2%)
    reduce_scatter x1, waiting for transfers between devices, shards(): lax.psum_scatter(partial_gate.astype(jnp.bfloat16), 'dp', scatter_dimensi...  124 us
    reduce_scatter x1, waiting for transfers between devices, shards(): lax.psum_scatter(partial_up.astype(jnp.bfloat16), 'dp', scatter_dimension...  124 us
    all_gather x1, waiting for transfers between devices, shards(): lax.all_gather(mate_shares[0], 'dp', axis=0, tiled=True)  79.6 us
    all_gather x1, waiting for transfers between devices, shards(): lax.all_gather(mate_shares[2], 'dp', axis=1, tiled=True)  79 us
    reduce_scatter x1, waiting for transfers between devices, shards(): lax.psum_scatter(partial_down.astype(jnp.bfloat16), 'dp', scatter_dimensi...  45 us
    all_gather x1, waiting for transfers between devices, shards(): lax.all_gather(mate_shares[1], 'dp', axis=0, tiled=True)  34.6 us
    all_to_all x2, blocking collectives, shards(): lax.all_to_all(as_sent(outgoing), 'expert', split_axis=0, concat_axis=0,...  29.2 us
    all_to_all x1, waiting for transfers between devices, shards(): lax.all_to_all(expert_out.reshape(groups, capacity, model_width), 'expert...  15.8 us
  transfers between devices with their start and end apart: 11, of which 10 were waited for; matrix products, arithmetic and copies ran while one was open for 10% of the time, Pallas kernels for 0%

commit v1 on v0

--- a/solution.py
+++ b/solution.py
@@ -2,6 +2,7 @@
 import jax.numpy as jnp
 from jax import lax
 from jax.sharding import PartitionSpec as P
+from jax.lax import all_to_all, axis_size
 
 
 def as_sent(shard):
@@ -68,8 +69,11 @@
         outgoing,
     )
     mate_shares = tuple((pick_from(block_piece, my_mate) for block_piece in incoming))
+    expand_the_notes = lambda in_array, axis_id: jnp.concatenate(
+        all_to_all(jnp.stack([in_array for _ in range(axis_size(axis_id))]), axis_id, 0, 0), axis=0
+    )
     gate_mat, up_mat, down_mat = (
-        lax.all_gather(mate_shares[0], "dp", axis=0, tiled=True),
+        expand_the_notes(mate_shares[0], "dp"),
         lax.all_gather(mate_shares[1], "dp", axis=0, tiled=True),
         lax.all_gather(mate_shares[2], "dp", axis=1, tiled=True),
     )

time: 689 us -> 626 us (0.909)
  waiting for transfers between devices: 529 us -> 468 us
  blocking collectives: 29.2 us -> 0 us
  starting transfers between devices: 32.2 us -> 55.7 us
    all_gather x1 -> x0, waiting for transfers between devices: 79.6 us -> none  [shards(): lax.all_gather(mate_shares[0], 'dp', axis=0, tiled=True)]
    all_to_all x0 -> x1, waiting for transfers between devices: none -> 72.3 us  [shards(): all_to_all(jnp.stack([in_array for _ in range(axis_size(axis_id))]), axis...]
    all_gather x1, waiting for transfers between devices: 79 us -> 26.6 us  [shards(): lax.all_gather(mate_shares[2], 'dp', axis=1, tiled=True)]
    all_gather x1, waiting for transfers between devices: 34.6 us -> 0.02 us  [shards(): lax.all_gather(mate_shares[1], 'dp', axis=0, tiled=True)]
    all_to_all x2 -> x0, blocking collectives: 29.2 us -> none  [shards(): lax.all_to_all(as_sent(outgoing), 'expert', split_axis=0, concat_axis=0,...]
    all_to_all x1 -> x3, waiting for transfers between devices: 7.28 us -> 20.6 us  [shards(): lax.all_to_all(as_sent(outgoing), 'expert', split_axis=0, concat_axis=0,...]
    all_to_all x1 -> x3, starting transfers between devices: 6.32 us -> 18.4 us  [shards(): lax.all_to_all(as_sent(outgoing), 'expert', split_axis=0, concat_axis=0,...]
    all_to_all x0 -> x1, starting transfers between devices: none -> 12 us  [shards(): all_to_all(jnp.stack([in_array for _ in range(axis_size(axis_id))]), axis...]
  transfers between devices with their start and end apart: 11 -> 13, of which waited for: 10 -> 12; matrix products, arithmetic and copies ran while one was open for 10% -> 11% of each run, Pallas kernels for 0% -> 0%
where the time goes in v1:
time: 626 us; the launch traced here: 625 us
  waiting for transfers between devices  468 us (75%)
  starting transfers between devices  55.7 us (9%)
  matrix products  37.7 us (6%)
  local copies, waits for them, and re-layouts  25.2 us (4%)
  other arithmetic  22.4 us (4%)
  between operations  15.9 us (3%)
    reduce_scatter x1, waiting for transfers between devices, shards(): lax.psum_scatter(partial_gate.astype(jnp.bfloat16), 'dp', scatter_dimensi...  124 us
    reduce_scatter x1, waiting for transfers between devices, shards(): lax.psum_scatter(partial_up.astype(jnp.bfloat16), 'dp', scatter_dimension...  124 us
    all_to_all x1, waiting for transfers between devices, shards(): all_to_all(jnp.stack([in_array for _ in range(axis_size(axis_id))]), axis...  72.3 us
    reduce_scatter x1, waiting for transfers between devices, shards(): lax.psum_scatter(partial_down.astype(jnp.bfloat16), 'dp', scatter_dimensi...  45.9 us
    all_gather x1, waiting for transfers between devices, shards(): lax.all_gather(mate_shares[2], 'dp', axis=1, tiled=True)  26.6 us
    all_to_all x3, waiting for transfers between devices, shards(): lax.all_to_all(as_sent(outgoing), 'expert', split_axis=0, concat_axis=0,...  20.6 us
    all_to_all x3, starting transfers between devices, shards(): lax.all_to_all(as_sent(outgoing), 'expert', split_axis=0, concat_axis=0,...  18.4 us
    all_to_all x1, waiting for transfers between devices, shards(): lax.all_to_all(expert_out.reshape(groups, capacity, model_width), 'expert...  14.7 us
  transfers between devices with their start and end apart: 13, of which 12 were waited for; matrix products, arithmetic and copies ran while one was open for 11% of the time, Pallas kernels for 0%

profile of v1, /device:TPU:4, one launch (start us, length us, event | category | flops | bytes accessed | tf_op | source)
XLA Modules:
  0.0 624.6 jit_solution(2728377487406714974)
XLA Ops:
  10.4 6.5 %all-to-all-start.3 = ((bf16[8,64,768]{2,1,0:T(8,128)(2,1)}), bf16[8,64,768]{2,1,0:T(8,128)(2,1)}, u32[]{:S(2)}, u32[]{:S(2)}) async-start(bf16[8,64,768]{2,1,0:T(8,128)(2,1)} %get-tuple-element.33), calls=%async_computation.3 | async-start | bytes 1572864 | tf_op jit(solution)/shard_map/all_to_all | solution.py:68
  19.4 7.3 %all-to-all-done.3 = bf16[8,64,768]{2,1,0:T(8,128)(2,1)} async-done(((bf16[8,64,768]{2,1,0:T(8,128)(2,1)}), bf16[8,64,768]{2,1,0:T(8,128)(2,1)}, u32[]{:S(2)}, u32[]{:S(2)}) %all-to-all-start.3) | async-done | bytes 786464 | tf_op jit(solution)/shard_map/all_to_all | solution.py:68
  28.3 6.3 %all-to-all-start.1 = ((bf16[8,64,768]{2,1,0:T(8,128)(2,1)}), bf16[8,64,768]{2,1,0:T(8,128)(2,1)}, u32[]{:S(2)}, u32[]{:S(2)}) async-start(bf16[8,64,768]{2,1,0:T(8,128)(2,1)} %get-tuple-element.32), calls=%async_computation.1 | async-start | bytes 1572864 | tf_op jit(solution)/shard_map/all_to_all | solution.py:68
  36.8 6.8 %all-to-all-done.1 = bf16[8,64,768]{2,1,0:T(8,128)(2,1)} async-done(((bf16[8,64,768]{2,1,0:T(8,128)(2,1)}), bf16[8,64,768]{2,1,0:T(8,128)(2,1)}, u32[]{:S(2)}, u32[]{:S(2)}) %all-to-all-start.1) | async-done | bytes 786464 | tf_op jit(solution)/shard_map/all_to_all | solution.py:68
  43.6 5.6 all-to-all-start.4
  52.3 6.5 %all-to-all-done.4 = bf16[8,768,64]{1,2,0:T(8,128)(2,1)S(1)} async-done(((bf16[8,768,64]{1,2,0:T(8,128)(2,1)}), bf16[8,768,64]{1,2,0:T(8,128)(2,1)S(1)}, u32[]{:S(2)}, u32[]{:S(2)}) %all-to-all-start.4) | async-done | bytes 786464 | tf_op jit(solution)/shard_map/all_to_all | solution.py:68
  58.8 5.7 all-to-all-start
  65.4 14.3 %all-to-all-done = bf16[8,40,2048]{2,1,0:T(8,128)(2,1)S(1)} async-done(((bf16[8,40,2048]{2,1,0:T(8,128)(2,1)}), bf16[8,40,2048]{2,1,0:T(8,128)(2,1)S(1)}, u32[]{:S(2)}, u32[]{:S(2)}) %all-to-all-start) | async-done | bytes 1310752 | tf_op jit(solution)/shard_map/all_to_all | solution.py:84
  81.9 12.0 %all-to-all-start.2 = ((bf16[32,64,768]{2,1,0:T(8,128)(2,1)}), bf16[32,64,768]{2,1,0:T(8,128)(2,1)}, u32[]{:S(2)}, u32[]{:S(2)}) async-start(bf16[32,64,768]{2,1,0:T(8,128)(2,1)} %stack.2), calls=%async_computation.2 | async-start | bytes 6291456 | tf_op jit(solution)/shard_map/all_to_all | solution.py:73
  97.1 2.7 mul.84
  101.7 72.3 %all-to-all-done.2 = bf16[32,64,768]{2,1,0:T(8,128)(2,1)} async-done(((bf16[32,64,768]{2,1,0:T(8,128)(2,1)}), bf16[32,64,768]{2,1,0:T(8,128)(2,1)}, u32[]{:S(2)}, u32[]{:S(2)}) %all-to-all-start.2) | async-done | bytes 3145760 | tf_op jit(solution)/shard_map/all_to_all | solution.py:73
  174.0 7.0 %all-to-all-start.6 = ((bf16[8,40,2048]{2,1,0:T(8,128)(2,1)}), bf16[8,40,2048]{2,1,0:T(8,128)(2,1)}, u32[]{:S(2)}, u32[]{:S(2)}) async-start(bf16[8,40,2048]{2,1,0:T(8,128)(2,1)} %bitcast.70), calls=%async_computation.6 | async-start | bytes 2621440 | tf_op jit(solution)/shard_map/all_to_all | solution.py:119
  181.0 3.9 fusion.23
  184.9 4.0 fusion.6
  188.9 11.8 %all-to-all-done.6 = bf16[8,40,2048]{2,1,0:T(8,128)(2,1)} async-done(((bf16[8,40,2048]{2,1,0:T(8,128)(2,1)}), bf16[8,40,2048]{2,1,0:T(8,128)(2,1)}, u32[]{:S(2)}, u32[]{:S(2)}) %all-to-all-start.6) | async-done | bytes 1310752 | tf_op jit(solution)/shard_map/all_to_all | solution.py:119
  200.7 26.6 %all-gather.7.cloned.1.call-done = bf16[1,768,2048]{1,2,0:T(8,128)(2,1)} async-done(((bf16[1,768,64]{1,2,0:T(8,128)(2,1)}), bf16[1,768,2048]{1,2,0:T(8,128)(2,1)}) %all-gather.7.cloned.1.call-update) | async-done | bytes 3145744 | tf_op jit(solution)/shard_map/all_gather | solution.py:78
  227.3 4.7 multiply_convert_fusion.2
  232.8 4.8 convolution_convert_fusion
  238.7 3.5 convolution_convert_fusion.1
  242.3 3.6 convolution_convert_fusion.2
  245.9 3.5 fusion.24
  251.7 5.2 all-to-all-start.7
  256.9 4.2 fusion.14
  261.1 12.7 %all-to-all-done.7 = bf16[8,40,2048]{2,1,0:T(8,128)(2,1)S(1)} async-done(((bf16[8,40,2048]{2,1,0:T(8,128)(2,1)}), bf16[8,40,2048]{2,1,0:T(8,128)(2,1)S(1)}, u32[]{:S(2)}, u32[]{:S(2)}) %all-to-all-start.7) | async-done | bytes 1310752 | tf_op jit(solution)/shard_map/all_to_all | solution.py:134
  273.8 7.2 %all-to-all-start.5 = ((bf16[8,40,2048]{2,1,0:T(8,128)(2,1)}), bf16[8,40,2048]{2,1,0:T(8,128)(2,1)S(1)}, u32[]{:S(2)}, u32[]{:S(2)}) async-start(bf16[8,40,2048]{2,1,0:T(8,128)(2,1)} %bitcast.75), calls=%async_computation.5 | async-start | bytes 2621440 | tf_op jit(solution)/shard_map/all_to_all | solution.py:96
  283.4 14.7 %all-to-all-done.5 = bf16[8,40,2048]{2,1,0:T(8,128)(2,1)S(1)} async-done(((bf16[8,40,2048]{2,1,0:T(8,128)(2,1)}), bf16[8,40,2048]{2,1,0:T(8,128)(2,1)S(1)}, u32[]{:S(2)}, u32[]{:S(2)}) %all-to-all-start.5) | async-done | bytes 1310752 | tf_op jit(solution)/shard_map/all_to_all | solution.py:96
  299.4 2.9 broadcast_select_fusion
  308.4 4.7 reduce.1
  313.2 5.6 multiply_reduce_fusion.1
  318.8 45.9 %reduce-scatter.8.cloned.1.call-done = bf16[768,64]{0,1:T(8,128)(2,1)} async-done(((bf16[768,2048]{0,1:T(8,128)(2,1)}), bf16[768,64]{0,1:T(8,128)(2,1)}) %reduce-scatter.8.cloned.1.call-update) | async-done | bytes 98320 | tf_op jit(solution)/shard_map/reduce_scatter | solution.py:157
  366.2 124.3 %reduce-scatter.6.cloned.1.call-done = bf16[64,768]{1,0:T(8,128)(2,1)} async-done(((bf16[2048,768]{1,0:T(8,128)(2,1)}), bf16[64,768]{1,0:T(8,128)(2,1)}) %reduce-scatter.6.cloned.1.call-update) | async-done | bytes 98320 | tf_op jit(solution)/shard_map/reduce_scatter | solution.py:154
  492.1 124.3 %reduce-scatter.4.cloned.1.call-done = bf16[64,768]{1,0:T(8,128)(2,1)} async-done(((bf16[2048,768]{1,0:T(8,128)(2,1)}), bf16[64,768]{1,0:T(8,128)(2,1)}) %reduce-scatter.4.cloned.1.call-update) | async-done | bytes 98320 | tf_op jit(solution)/shard_map/reduce_scatter | solution.py:151
  (90 shorter events, 37.6 us)
Async XLA Ops:
  7.2 28.3 %copy-start = (bf16[1,768,2048]{2,1,0:T(8,128)(2,1)S(1)}, bf16[1,768,2048]{2,1,0:T(8,128)(2,1)}, u32[]{:S(2)}) copy-start(bf16[1,768,2048]{2,1,0:T(8,128)(2,1)} %param.17) | copy-start | bytes 9437188
  7.2 9.7 %copy-start.12 = (s32[8]{0:T(128)S(1)}, s32[8]{0:T(128)}, u32[]{:S(2)}) copy-start(s32[8]{0:T(128)} %param.14) | copy-start | bytes 100
  10.4 24.1 %copy-start.10 = (s32[128,2]{0,1:T(2,128)S(1)}, s32[128,2]{0,1:T(2,128)}, u32[]{:S(2)}) copy-start(s32[128,2]{0,1:T(2,128)} %param.12) | copy-start | bytes 3076
  10.4 16.3 %all-to-all-start.3 = ((bf16[8,64,768]{2,1,0:T(8,128)(2,1)}), bf16[8,64,768]{2,1,0:T(8,128)(2,1)}, u32[]{:S(2)}, u32[]{:S(2)}) async-start(bf16[8,64,768]{2,1,0:T(8,128)(2,1)} %get-tuple-element.33), calls=%async_computation.3 | async-start | bytes 1572864 | tf_op jit(solution)/shard_map/all_to_all | solution.py:68
  16.9 168.0 %all-gather.5.cloned.1.call-start = ((), (), s32[]{:S(2)}) async-start(), calls=%async_computation.14 | async-start | bytes 3244032 | tf_op jit(solution)/shard_map/all_gather | solution.py:77
  28.3 15.3 %all-to-all-start.1 = ((bf16[8,64,768]{2,1,0:T(8,128)(2,1)}), bf16[8,64,768]{2,1,0:T(8,128)(2,1)}, u32[]{:S(2)}, u32[]{:S(2)}) async-start(bf16[8,64,768]{2,1,0:T(8,128)(2,1)} %get-tuple-element.32), calls=%async_computation.1 | async-start | bytes 1572864 | tf_op jit(solution)/shard_map/all_to_all | solution.py:68
  35.6 13.9 %copy-start.8 = (bf16[128,2048]{1,0:T(8,128)(2,1)S(1)}, bf16[128,2048]{1,0:T(8,128)(2,1)}, u32[]{:S(2)}) copy-start(bf16[128,2048]{1,0:T(8,128)(2,1)} %param.10) | copy-start | bytes 1572868
  43.6 15.2 %all-to-all-start.4 = ((bf16[8,768,64]{1,2,0:T(8,128)(2,1)}), bf16[8,768,64]{1,2,0:T(8,128)(2,1)S(1)}, u32[]{:S(2)}, u32[]{:S(2)}) async-start(bf16[8,768,64]{1,2,0:T(8,128)(2,1)} %broadcast_select_fusion.1), calls=%async_computation.4 | async-start | bytes 1572864 | tf_op jit(solution)/shard_map/all_to_all | solution.py:68
  58.8 20.9 %all-to-all-start = ((bf16[8,40,2048]{2,1,0:T(8,128)(2,1)}), bf16[8,40,2048]{2,1,0:T(8,128)(2,1)S(1)}, u32[]{:S(2)}, u32[]{:S(2)}) async-start(bf16[8,40,2048]{2,1,0:T(8,128)(2,1)} %bitcast.3), calls=%async_computation | async-start | bytes 2621440 | tf_op jit(solution)/shard_map/all_to_all | solution.py:84
  79.7 2.2 copy-start.6
  81.9 12.7 %copy-start.9 = (bf16[128,2048]{1,0:T(8,128)(2,1)S(1)}, bf16[128,2048]{1,0:T(8,128)(2,1)}, u32[]{:S(2)}) copy-start(bf16[128,2048]{1,0:T(8,128)(2,1)} %param.11) | copy-start | bytes 1572868
  81.9 92.1 %all-to-all-start.2 = ((bf16[32,64,768]{2,1,0:T(8,128)(2,1)}), bf16[32,64,768]{2,1,0:T(8,128)(2,1)}, u32[]{:S(2)}, u32[]{:S(2)}) async-start(bf16[32,64,768]{2,1,0:T(8,128)(2,1)} %stack.2), calls=%async_computation.2 | async-start | bytes 6291456 | tf_op jit(solution)/shard_map/all_to_all | solution.py:73
  93.9 133.4 %all-gather.7.cloned.1.call-start = ((), (), s32[]{:S(2)}) async-start(), calls=%async_computation.15 | async-start | bytes 3244032 | tf_op jit(solution)/shard_map/all_gather | solution.py:78
  97.1 2.7 copy-start.11
  99.8 74.2 %copy-start.2 = (f32[256,2048]{1,0:T(8,128)}, f32[256,2048]{1,0:T(8,128)S(1)}, u32[]{:S(2)}) copy-start(f32[256,2048]{1,0:T(8,128)S(1)} %mul.84) | copy-start | bytes 6291460
  174.0 26.7 %all-to-all-start.6 = ((bf16[8,40,2048]{2,1,0:T(8,128)(2,1)}), bf16[8,40,2048]{2,1,0:T(8,128)(2,1)}, u32[]{:S(2)}, u32[]{:S(2)}) async-start(bf16[8,40,2048]{2,1,0:T(8,128)(2,1)} %bitcast.70), calls=%async_computation.6 | async-start | bytes 2621440 | tf_op jit(solution)/shard_map/all_to_all | solution.py:119
  181.0 183.7 %reduce-scatter.8.cloned.1.call-start = ((), (), s32[]{:S(2)}) async-start(), calls=%async_computation.13 | async-start | bytes 3244032 | tf_op jit(solution)/shard_map/reduce_scatter | solution.py:157
  181.0 3.9 copy-start.7
  232.0 0.8 copy-start.17
  232.0 10.2 %copy-start.14 = (bf16[320,768]{1,0:T(8,128)(2,1)}, bf16[320,768]{1,0:T(8,128)(2,1)S(1)}, u32[]{:S(2)}) copy-start(bf16[320,768]{1,0:T(8,128)(2,1)S(1)} %get-tuple-element.28) | copy-start | bytes 1474564
  237.7 1.0 copy-start.15
  237.7 252.9 %reduce-scatter.6.cloned.1.call-start = ((), (), s32[]{:S(2)}) async-start(), calls=%async_computation.12 | async-start | bytes 3244032 | tf_op jit(solution)/shard_map/reduce_scatter | solution.py:154
  242.2 374.2 %reduce-scatter.4.cloned.1.call-start = ((), (), s32[]{:S(2)}) async-start(), calls=%async_computation.11 | async-start | bytes 3244032 | tf_op jit(solution)/shard_map/reduce_scatter | solution.py:151
  245.9 3.5 copy-start.13
  245.9 3.5 copy-start.16
  251.7 5.2 copy-start.18
  251.7 22.1 %all-to-all-start.7 = ((bf16[8,40,2048]{2,1,0:T(8,128)(2,1)}), bf16[8,40,2048]{2,1,0:T(8,128)(2,1)S(1)}, u32[]{:S(2)}, u32[]{:S(2)}) async-start(bf16[8,40,2048]{2,1,0:T(8,128)(2,1)} %bitcast.17), calls=%async_computation.7 | async-start | bytes 2621440 | tf_op jit(solution)/shard_map/all_to_all | solution.py:134
  273.8 24.3 %all-to-all-start.5 = ((bf16[8,40,2048]{2,1,0:T(8,128)(2,1)}), bf16[8,40,2048]{2,1,0:T(8,128)(2,1)S(1)}, u32[]{:S(2)}, u32[]{:S(2)}) async-start(bf16[8,40,2048]{2,1,0:T(8,128)(2,1)} %bitcast.75), calls=%async_computation.5 | async-start | bytes 2621440 | tf_op jit(solution)/shard_map/all_to_all | solution.py:96
  299.4 2.9 copy-start.4
  302.3 4.9 copy-start.5
  304.5 2.7 copy-start.3
  308.4 309.6 %copy-start.1 = (bf16[1,768,2048]{2,1,0:T(8,128)(2,1)S(1)}, bf16[1,768,2048]{2,1,0:T(8,128)(2,1)}, u32[]{:S(2)}) copy-start(bf16[1,768,2048]{2,1,0:T(8,128)(2,1)} %param.17) | copy-start | bytes 9437188
Sparse Core Ops, SparseCore 0:
  28.4 92.7 all-gather.4
  124.5 102.7 all-gather.6
  237.8 126.8 reduce-scatter.7
  368.7 121.8 reduce-scatter.5
  494.6 121.8 reduce-scatter.3
